TPU v7x, 32 devices: a whole 2x2x4 slice. The times are simulated.
32 devices in a mesh: dp: 2 (over x), row: 4 (over y, core), col: 4 (over z).
Axes of the slice: x: 2, y: 2, z: 4, core: 2. Of those that a mesh axis runs over, the one named last changes fastest.
Arguments:
- tokens: bfloat16 [768, 39200], P('row', ('dp', 'col')), may hold values from -6 to 6
- grad_out: bfloat16 [768, 39200], P('row', ('dp', 'col')), may hold values from -6 to 6
- adapter_index: int32 [8, 1], replicated, may hold values from 0 to 7
- norm1_gain: bfloat16 [768], P('row'), may hold values from 0.099609375 to 1.8984375
- norm2_gain: bfloat16 [768], P('row'), may hold values from 0.099609375 to 1.8984375
- qkv_weight: bfloat16 [768, 2304], P('row', 'col'), may hold values from -0.21875 to 0.21875
- proj_weight: bfloat16 [768, 768], P('col', 'row'), may hold values from -0.875 to 0.875
- fc1_weight: bfloat16 [768, 3072], P('row', 'col'), may hold values from -0.21875 to 0.21875
- fc2_weight: bfloat16 [768, 3072], P('row', 'col'), may hold values from -0.109375 to 0.109375
- rel_h: bfloat16 [27, 64], replicated, may hold values from -0.59765625 to 0.59765625
- rel_w: bfloat16 [27, 64], replicated, may hold values from -0.59765625 to 0.59765625
- qkv_down: bfloat16 [8, 768, 16], P(None, 'row'), may hold values from -0.21875 to 0.21875
- qkv_up: bfloat16 [8, 16, 2304], P(None, None, 'col'), may hold values from -0.75 to 0.75
- proj_down: bfloat16 [8, 768, 16], P(None, 'col'), may hold values from -0.21875 to 0.21875
- proj_up: bfloat16 [8, 16, 768], P(None, None, 'row'), may hold values from -0.75 to 0.75
- fc1_down: bfloat16 [8, 768, 16], P(None, 'row'), may hold values from -0.21875 to 0.21875
- fc1_up: bfloat16 [8, 16, 3072], P(None, None, 'col'), may hold values from -0.75 to 0.75
- fc2_down: bfloat16 [8, 3072, 16], P(None, 'col'), may hold values from -0.109375 to 0.109375
- fc2_up: bfloat16 [8, 16, 768], P(None, None, 'row'), may hold values from -0.75 to 0.75
Outputs:
- out: bfloat16 [768, 39200], P('row', ('dp', 'col'))
- tokens_grad: float32 [768, 39200], P('row', ('dp', 'col'))
- qkv_down_grad: float32 [8, 768, 16], P(None, 'row')
- qkv_up_grad: float32 [8, 16, 2304], P(None, None, 'col')
- proj_down_grad: float32 [8, 768, 16], P(None, 'col')
- proj_up_grad: float32 [8, 16, 768], P(None, None, 'row')
- fc1_down_grad: float32 [8, 768, 16], P(None, 'row')
- fc1_up_grad: float32 [8, 16, 3072], P(None, None, 'col')
- fc2_down_grad: float32 [8, 3072, 16], P(None, 'col')
- fc2_up_grad: float32 [8, 16, 768], P(None, None, 'row')
Inputs may be any that keep to these rules, and one draw needn't show every extreme that they name: `adapter_index`: every one of the 8 adapters is chosen by at least one image.
All inputs are finite; a program needn't handle non-finite values.
Results may differ from a plain program's by a relative error of at most 0.015.
Values may be sent and summed in bfloat16 or wider, within the bound.
No kernel may reach another device: no remote copies, remote signals or barrier semaphores. Data moves between devices by JAX's collectives and lax.ppermute only.
A program may use at most 448 MiB of HBM per device.

v0:
```python
import jax
import jax.numpy as jnp
from jax import lax
from jax.sharding import PartitionSpec as P

D = 768
HD = 64
WIN = 14
SIDE = 64
ADAPT = 8
NWIN_SIDE = 5
IMG_TOK = 4900
PRECISE = lax.Precision.HIGHEST
EPSILON = 1e-06


def exact_gelu(values):
    return jax.nn.gelu(values, approximate=False)


def valid_rows():
    position = jnp.arange(IMG_TOK, dtype=jnp.int32)
    window = position // (WIN * WIN)
    inside = position % (WIN * WIN)
    image_row = window // NWIN_SIDE * WIN + inside // WIN
    image_col = window % NWIN_SIDE * WIN + inside % WIN
    return ((image_row < SIDE) & (image_col < SIDE)).astype(jnp.float32)


def rel_table(rel_param):
    offsets = (
        jnp.arange(WIN, dtype=jnp.int32)[:, None]
        - jnp.arange(WIN, dtype=jnp.int32)[None, :]
        + WIN
        - 1
    )
    one_hot = (
        offsets[:, :, None] == jnp.arange(2 * WIN - 1, dtype=jnp.int32)[None, None, :]
    ).astype(jnp.bfloat16)
    return jnp.einsum("akn,nc->akc", one_hot, rel_param, preferred_element_type=jnp.float32).astype(
        jnp.bfloat16
    )


def pick_one(adapter, own_pick):
    return jnp.einsum("a,ade->de", own_pick, adapter.astype(jnp.float32), precision=PRECISE).astype(
        jnp.bfloat16
    )


def row_totals(first_sum, second_sum):
    return lax.psum((first_sum, second_sum), "row")


def norm_forward(values):
    totals = row_totals(jnp.sum(values, axis=1), jnp.sum(values * values, axis=1))
    center = totals[0] / D
    inv_std = lax.rsqrt(totals[1] / D - center * center + EPSILON)
    return ((values - center[:, None]) * inv_std[:, None], inv_std)


def norm_backward(grad_normed, normed, inv_std):
    totals = row_totals(jnp.sum(grad_normed, axis=1), jnp.sum(grad_normed * normed, axis=1))
    return inv_std[:, None] * (
        grad_normed - totals[0][:, None] / D - normed * totals[1][:, None] / D
    )


def local_norm(values):
    center = jnp.sum(values, axis=1) / D
    inv_std = lax.rsqrt(jnp.sum(values * values, axis=1) / D - center * center + EPSILON)
    return ((values - center[:, None]) * inv_std[:, None], inv_std)


def local_norm_back(grad_normed, normed, inv_std):
    first_mean = jnp.sum(grad_normed, axis=1) / D
    second_mean = jnp.sum(grad_normed * normed, axis=1) / D
    return inv_std[:, None] * (grad_normed - first_mean[:, None] - normed * second_mean[:, None])


def to_features(values):
    return lax.all_to_all(
        values.astype(jnp.bfloat16), "row", split_axis=0, concat_axis=1, tiled=True
    ).astype(values.dtype)


def to_tokens(values):
    return lax.all_to_all(
        values.astype(jnp.bfloat16), "row", split_axis=1, concat_axis=0, tiled=True
    ).astype(values.dtype)


def token_rows(values):
    return lax.all_to_all(values, "row", split_axis=0, concat_axis=1, tiled=True)


def head_cols(values):
    return lax.all_to_all(values, "row", split_axis=1, concat_axis=0, tiled=True)


def head_sums(values):
    return lax.all_to_all(
        values.astype(jnp.bfloat16), "row", split_axis=1, concat_axis=0, tiled=True
    ).astype(values.dtype)


def adapted_local(inputs, weight, down_mat, up_mat):
    product = jnp.dot(inputs, weight, preferred_element_type=jnp.float32)
    reduced = jnp.dot(inputs, down_mat, preferred_element_type=jnp.float32)
    return product + jnp.dot(reduced, up_mat.astype(jnp.float32), precision=PRECISE)


def adapted_back(grads, weight, down_mat, up_mat):
    contract = (((1,), (1,)), ((), ()))
    product = lax.dot_general(grads, weight, contract, preferred_element_type=jnp.float32)
    reduced = lax.dot_general(grads, up_mat, contract, preferred_element_type=jnp.float32)
    return product + lax.dot_general(
        reduced, down_mat.astype(jnp.float32), contract, precision=PRECISE
    )


def pair_grads(inputs_m, grads_m, down_m, up_m):
    reduced = jnp.dot(inputs_m, down_m, preferred_element_type=jnp.float32)
    back_red = lax.dot_general(
        grads_m, up_m, (((1,), (1,)), ((), ())), preferred_element_type=jnp.float32
    )
    grad_down = jnp.einsum("td,tr->dr", inputs_m, back_red, precision=PRECISE)
    grad_up = jnp.einsum("tr,to->ro", reduced, grads_m, precision=PRECISE)
    return (grad_down, grad_up)


def spread_pick(own_pick, grad_mat):
    return jnp.einsum("a,de->ade", own_pick, grad_mat)


def take_block(full, dim, index, length):
    return lax.dynamic_slice_in_dim(full, index * length, length, dim)


def split_qkv(qkv_low):
    heads_local = qkv_low.shape[1] // (3 * HD)
    arranged = qkv_low.reshape(NWIN_SIDE * NWIN_SIDE, WIN * WIN, heads_local, 3, HD)
    return (arranged[:, :, :, 0], arranged[:, :, :, 1], arranged[:, :, :, 2])


def score_matrix(query_b, key_b, tables):
    windows = query_b.shape[0]
    heads_local = query_b.shape[2]
    dot_scores = jnp.einsum(
        "nqhc,nkhc->nhqk", query_b, key_b, preferred_element_type=jnp.float32
    ) * HD ** (-0.5)
    spatial = query_b.reshape(windows, WIN, WIN, heads_local, HD)
    rel_rows = jnp.einsum(
        "nabhc,akc->nhabk", spatial, tables[0], preferred_element_type=jnp.float32
    )
    rel_cols = jnp.einsum(
        "nabhc,bkc->nhabk", spatial, tables[1], preferred_element_type=jnp.float32
    )
    shaped = dot_scores.reshape(windows, heads_local, WIN, WIN, WIN, WIN)
    shaped = shaped + rel_rows[:, :, :, :, :, None] + rel_cols[:, :, :, :, None, :]
    return shaped.reshape(windows, heads_local, WIN * WIN, WIN * WIN)


def attend(qkv_low, tables):
    query_b, key_b, value_b = split_qkv(qkv_low)
    scores = score_matrix(query_b, key_b, tables)
    maxima = jnp.max(scores, axis=3, keepdims=True)
    exponent = jnp.exp(scores - maxima)
    sum_exp = jnp.sum(exponent, axis=3, keepdims=True)
    attn_prob = (exponent / sum_exp).astype(jnp.bfloat16)
    attended = jnp.einsum("nhqk,nkhc->nqhc", attn_prob, value_b, preferred_element_type=jnp.float32)
    log_total = (maxima + jnp.log(sum_exp))[:, :, :, 0]
    return (attended.reshape(IMG_TOK, attended.shape[2] * HD).astype(jnp.bfloat16), log_total)


def attend_back(qkv_low, log_total, grad_attended, tables):
    query_b, key_b, value_b = split_qkv(qkv_low)
    windows = query_b.shape[0]
    heads_local = query_b.shape[2]
    scores = score_matrix(query_b, key_b, tables)
    attn_exact = jnp.exp(scores - log_total[:, :, :, None])
    prob_low = attn_exact.astype(jnp.bfloat16)
    grad_o = grad_attended.reshape(windows, WIN * WIN, heads_local, HD)
    grad_v = jnp.einsum("nhqk,nqhc->nkhc", prob_low, grad_o, preferred_element_type=jnp.float32)
    grad_p = jnp.einsum("nqhc,nkhc->nhqk", grad_o, value_b, preferred_element_type=jnp.float32)
    centre = jnp.sum(grad_p * attn_exact, axis=3, keepdims=True)
    grad_s = (attn_exact * (grad_p - centre)).astype(jnp.bfloat16)
    grad_q = jnp.einsum(
        "nhqk,nkhc->nqhc", grad_s, key_b, preferred_element_type=jnp.float32
    ) * HD ** (-0.5)
    grad_k = jnp.einsum(
        "nhqk,nqhc->nkhc", grad_s, query_b, preferred_element_type=jnp.float32
    ) * HD ** (-0.5)
    split_grad = grad_s.astype(jnp.float32).reshape(windows, heads_local, WIN, WIN, WIN, WIN)
    along_rows = jnp.sum(split_grad, axis=5)
    along_cols = jnp.sum(split_grad, axis=4)
    rel_grad = jnp.einsum(
        "nhabk,akc->nabhc", along_rows, tables[0].astype(jnp.float32), precision=PRECISE
    )
    rel_grad = rel_grad + jnp.einsum(
        "nhabk,bkc->nabhc", along_cols, tables[1].astype(jnp.float32), precision=PRECISE
    )
    grad_q = grad_q + rel_grad.reshape(windows, WIN * WIN, heads_local, HD)
    stacked = jnp.stack([grad_q, grad_k, grad_v], axis=3)
    return stacked.reshape(IMG_TOK, heads_local * 3 * HD).astype(jnp.bfloat16)


def body(
    tokens,
    grad_out,
    adapter_index,
    norm1_gain,
    norm2_gain,
    qkv_weight,
    proj_weight,
    fc1_weight,
    fc2_weight,
    rel_h,
    rel_w,
    qkv_down,
    qkv_up,
    proj_down,
    proj_up,
    fc1_down,
    fc1_up,
    fc2_down,
    fc2_up,
):
    members = lax.axis_size("col")
    row_index = lax.axis_index("row")
    col_index = lax.axis_index("col")
    group_ids = lax.dynamic_slice_in_dim(
        adapter_index[:, 0], lax.axis_index("dp") * members, members, 0
    )
    chosen = (group_ids[:, None] == jnp.arange(ADAPT, dtype=jnp.int32)[None, :]).astype(jnp.float32)
    own_pick = chosen[col_index]
    validity = valid_rows()[:, None]
    tables = (rel_table(rel_h), rel_table(rel_w))
    inputs = tokens.astype(jnp.float32).T
    normed_one, inv_one = norm_forward(inputs)
    gain_one = norm1_gain.astype(jnp.float32)
    hidden_one = (normed_one * gain_one * validity).astype(jnp.bfloat16)
    qkv_part, proj_part, qkv_dn_part, proj_up_part = (
        lax.all_gather(qkv_weight, "row", axis=0, tiled=True),
        lax.all_gather(proj_weight, "row", axis=1, tiled=True),
        lax.all_gather(qkv_down, "row", axis=1, tiled=True),
        lax.all_gather(proj_up, "row", axis=2, tiled=True),
    )
    qkv_full, proj_full, qkv_up_all, proj_dn_all = (
        lax.all_gather(qkv_part, "col", axis=1, tiled=True),
        lax.all_gather(proj_part, "col", axis=0, tiled=True),
        lax.all_gather(qkv_up, "col", axis=2, tiled=True),
        lax.all_gather(proj_down, "col", axis=1, tiled=True),
    )
    qkv_dn = pick_one(qkv_dn_part, own_pick)
    qkv_upm = pick_one(qkv_up_all, own_pick)
    proj_dn = pick_one(proj_dn_all, own_pick)
    proj_upm = pick_one(proj_up_part, own_pick)
    hidden_rows = token_rows(hidden_one)
    qkv_rows_out = adapted_local(hidden_rows, qkv_full, qkv_dn, qkv_upm).astype(jnp.bfloat16)
    qkv_low = head_cols(qkv_rows_out)
    attended, log_total = attend(qkv_low, tables)
    attended_rows = token_rows(attended)
    branch = head_sums(adapted_local(attended_rows, proj_full, proj_dn, proj_upm))
    middle = inputs + branch
    grad_final = grad_out.astype(jnp.float32).T * validity
    weight_up, weight_stored, down_one, up_two, gain_full = (
        lax.all_gather(fc1_weight, "row", axis=0, tiled=True),
        lax.all_gather(fc2_weight, "row", axis=0, tiled=True),
        lax.all_gather(fc1_down, "row", axis=1, tiled=True),
        lax.all_gather(fc2_up, "row", axis=2, tiled=True),
        lax.all_gather(norm2_gain, "row", axis=0, tiled=True),
    )
    weight_up, weight_stored, up_one, down_two = (
        lax.all_gather(weight_up, "col", axis=1, tiled=True),
        lax.all_gather(weight_stored, "col", axis=1, tiled=True),
        lax.all_gather(fc1_up, "col", axis=2, tiled=True),
        lax.all_gather(fc2_down, "col", axis=1, tiled=True),
    )
    weight_down = weight_stored.T
    down_fc1 = pick_one(down_one, own_pick)
    up_fc1 = pick_one(up_one, own_pick)
    down_fc2 = pick_one(down_two, own_pick)
    up_fc2 = pick_one(up_two, own_pick)
    local_mid = to_features(middle)
    normed_two, inv_two = local_norm(local_mid)
    gain_two = gain_full.astype(jnp.float32)
    hidden_two = (normed_two * gain_two).astype(jnp.bfloat16)
    pre_act = adapted_local(hidden_two, weight_up, down_fc1, up_fc1)
    activated = exact_gelu(pre_act).astype(jnp.bfloat16)
    mlp_out = to_tokens(adapted_local(activated, weight_down, down_fc2, up_fc2))
    grad_local = to_features(grad_final).astype(jnp.bfloat16)
    grad_activ = adapted_back(grad_local, weight_down, down_fc2, up_fc2)
    gelu_value, gelu_back = jax.vjp(exact_gelu, pre_act)
    grad_pre = gelu_back(grad_activ)[0].astype(jnp.bfloat16)
    grad_hidden_two = adapted_back(grad_pre, weight_up, down_fc1, up_fc1)
    grad_middle = grad_final + to_tokens(
        local_norm_back(grad_hidden_two * gain_two, normed_two, inv_two)
    )
    fc1_local = pair_grads(hidden_two, grad_pre, down_fc1, up_fc1)
    fc2_local = pair_grads(activated, grad_local, down_fc2, up_fc2)
    summed_all = lax.psum(
        (
            spread_pick(own_pick, fc1_local[0]),
            spread_pick(own_pick, fc1_local[1]),
            spread_pick(own_pick, fc2_local[0]),
            spread_pick(own_pick, fc2_local[1]),
        ),
        ("dp", "row", "col"),
    )
    fc1_down_grad = take_block(summed_all[0], 1, row_index, fc1_down.shape[1])
    fc1_up_grad = take_block(summed_all[1], 2, col_index, fc1_up.shape[2])
    fc2_down_grad = take_block(summed_all[2], 1, col_index, fc2_down.shape[1])
    fc2_up_grad = take_block(summed_all[3], 2, row_index, fc2_up.shape[2])
    result = ((middle + mlp_out) * validity).astype(jnp.bfloat16).T
    grad_branch = grad_middle.astype(jnp.bfloat16)
    grad_branch_rows = token_rows(grad_branch)
    grad_attended = head_cols(
        adapted_back(grad_branch_rows, proj_full, proj_dn, proj_upm).astype(jnp.bfloat16)
    )
    grad_qkv = attend_back(qkv_low, log_total, grad_attended, tables)
    grad_qkv_rows = token_rows(grad_qkv)
    grad_hidden_one = head_sums(adapted_back(grad_qkv_rows, qkv_full, qkv_dn, qkv_upm))
    qkv_pair = pair_grads(hidden_rows, grad_qkv_rows, qkv_dn, qkv_upm)
    proj_pair = pair_grads(attended_rows, grad_branch_rows, proj_dn, proj_upm)
    attn_sums = lax.psum(
        (
            spread_pick(own_pick, qkv_pair[0]),
            spread_pick(own_pick, qkv_pair[1]),
            spread_pick(own_pick, proj_pair[0]),
            spread_pick(own_pick, proj_pair[1]),
        ),
        ("dp", "row", "col"),
    )
    qkv_down_grad = take_block(attn_sums[0], 1, row_index, qkv_down.shape[1])
    qkv_up_grad = take_block(attn_sums[1], 2, col_index, qkv_up.shape[2])
    proj_down_grad = take_block(attn_sums[2], 1, col_index, proj_down.shape[1])
    proj_up_grad = take_block(attn_sums[3], 2, row_index, proj_up.shape[2])
    grad_inputs = (
        grad_middle + norm_backward(grad_hidden_one * validity * gain_one, normed_one, inv_one)
    ).T
    return (
        result,
        grad_inputs,
        qkv_down_grad,
        qkv_up_grad,
        proj_down_grad,
        proj_up_grad,
        fc1_down_grad,
        fc1_up_grad,
        fc2_down_grad,
        fc2_up_grad,
    )


def solution(mesh):
    return jax.shard_map(
        body,
        mesh=mesh,
        in_specs=(
            P("row", ("dp", "col")),
            P("row", ("dp", "col")),
            P(),
            P("row"),
            P("row"),
            P("row", "col"),
            P("col", "row"),
            P("row", "col"),
            P("row", "col"),
            P(),
            P(),
            P(None, "row", None),
            P(None, None, "col"),
            P(None, "col", None),
            P(None, None, "row"),
            P(None, "row", None),
            P(None, None, "col"),
            P(None, "col", None),
            P(None, None, "row"),
        ),
        out_specs=(
            P("row", ("dp", "col")),
            P("row", ("dp", "col")),
            P(None, "row", None),
            P(None, None, "col"),
            P(None, "col", None),
            P(None, None, "row"),
            P(None, "row", None),
            P(None, None, "col"),
            P(None, "col", None),
            P(None, None, "row"),
        ),
        check_vma=False,
    )
```

profile of v0, /device:TPU:0, one launch (start us, length us, event | category | flops | bytes accessed | tf_op | source)
XLA Modules:
  0.0 1826.9 jit_solution(15166732212104624496)
XLA Ops:
  7.3 11.5 all_gather.51
  20.9 11.5 all-reduce.3
  46.7 118.0 %all_gather.54 = bf16[8,16,2304]{1,0,2:T(8,128)(2,1)} all-gather(bf16[8,16,576]{1,0,2:T(8,128)(2,1)S(1)} %copy.225), channel_id=1, replica_groups=mesh['dp'=2,'row'=4,'col'=4] {'col'}, dimensions={2}, use_global_device_ids=true | all-gather | bytes 737280 | tf_op jit(solution)/shard_map/all_gather | solution.py:252
  171.6 12.9 all_gather.62
  184.5 30.9 %all_gather.57 = bf16[8,768,16]{2,0,1:T(8,128)(2,1)S(1)} all-gather(bf16[8,192,16]{2,0,1:T(8,128)(2,1)} %copy.243), channel_id=1, replica_groups=mesh['dp'=2,'row'=4,'col'=4] {'col'}, dimensions={1}, use_global_device_ids=true | all-gather | bytes 245760 | tf_op jit(solution)/shard_map/all_gather | solution.py:253
  215.4 12.6 all_gather.53
  247.6 8.9 copy.226
  263.0 74.5 %all_gather.55 = bf16[192,768]{0,1:T(8,128)(2,1)S(1)} all-gather(bf16[192,192]{0,1:T(8,128)(2,1)S(1)} %copy.241), channel_id=1, replica_groups=mesh['dp'=2,'row'=4,'col'=4] {'row'}, dimensions={1}, use_global_device_ids=true | all-gather | bytes 368640 | tf_op jit(solution)/shard_map/all_gather | solution.py:245
  338.7 13.0 all_gather.58
  362.3 9.7 copy.227
  372.0 26.8 %reshape.211 = bf16[25,196,3,3,64]{1,0,4,3,2:T(8,128)(2,1)} reshape(bf16[4,1225,576]{1,0,2:T(4,128)(2,1)} %copy.227) | data formatting | bytes 11289600 | tf_op jit(solution)/shard_map/reshape | solution.py:142
  427.1 21.4 %add.271 = f32[25,3,14,14,14,14]{0,5,4,3,2,1:T(8,128)} broadcast(f32[25,3,14,14,14]{0,4,3,2,1:T(8,128)S(1)} %copy.236), dimensions={0,1,2,3,5} | broadcast | bytes 12348000 | tf_op jit(solution)/shard_map/add | solution.py:160
  448.6 64.5 %add.272 = f32[25,3,196,196]{0,3,2,1:T(8,128)} reshape(f32[25,3,14,14,14,14]{0,5,4,3,2,1:T(8,128)} %add.271) | data formatting | bytes 23049600 | tf_op jit(solution)/shard_map/add | solution.py:160
  513.1 39.1 %copy.237 = f32[25,3,196,196]{2,3,1,0:T(8,128)} copy(f32[25,3,196,196]{0,3,2,1:T(8,128)} %add.272) | data formatting | bytes 23049600 | tf_op jit(solution)/shard_map/add | solution.py:160
  563.4 22.8 %add.268 = f32[25,3,14,14,14,14]{0,5,4,3,2,1:T(8,128)} broadcast(f32[25,3,14,14,14]{0,4,3,2,1:T(8,128)} %copy.233), dimensions={0,1,2,3,4} | broadcast | bytes 12348000 | tf_op jit(solution)/shard_map/add | solution.py:160
  586.3 64.5 %add.269 = f32[25,3,196,196]{0,3,2,1:T(8,128)} reshape(f32[25,3,14,14,14,14]{0,5,4,3,2,1:T(8,128)} %add.268) | data formatting | bytes 23049600 | tf_op jit(solution)/shard_map/add | solution.py:160
  650.8 39.1 %copy.234 = f32[25,3,196,196]{2,3,1,0:T(8,128)} copy(f32[25,3,196,196]{0,3,2,1:T(8,128)} %add.269) | data formatting | bytes 23049600 | tf_op jit(solution)/shard_map/add | solution.py:160
  689.9 24.5 %fusion.132 = (f32[25,3,196]{2,1,0:T(4,128)S(1)}, f32[25,3,196,196]{2,3,1,0:T(8,128)}) fusion(f32[25,3,196,196]{2,3,1,0:T(8,128)} %copy.237, f32[25,3,196,196]{2,3,1,0:T(8,128)} %copy.234, bf16[25,196,3,1,64]{1,0,4,3,2:T(8,128)(2,1)} %get-tuple-element.37, bf16[25,196,3,1,64]{1,0,4,3,2:T(8,128)(2,1)S(1)} %copy-done.9), kind=kOutput, calls=%fused_computation.234 | convolution fusion | flops 380303744 | bytes 38396400 | tf_op jit(solution)/shard_map/nqhc,nkhc->nhqk/dot_general | solution.py:149
  714.4 9.8 fusion.6
  724.2 10.1 convert_bitcast_fusion.6
  763.8 10.6 all-to-all-done.2
  779.3 33.6 %all_gather.67 = bf16[8,16,768]{1,0,2:T(8,128)(2,1)S(1)} all-gather(bf16[8,16,192]{1,0,2:T(8,128)(2,1)} %copy.250), channel_id=1, replica_groups=mesh['dp'=2,'row'=4,'col'=4] {'row'}, dimensions={2}, use_global_device_ids=true | all-gather | bytes 245760 | tf_op jit(solution)/shard_map/all_gather | solution.py:271
  814.5 19.3 %all_gather.66 = bf16[8,3072,16]{1,2,0:T(8,128)(2,1)S(1)} all-gather(bf16[8,768,16]{1,2,0:T(8,128)(2,1)} %param.36), channel_id=1, replica_groups=mesh['dp'=2,'row'=4,'col'=4] {'col'}, dimensions={1}, use_global_device_ids=true | all-gather | bytes 983040 | tf_op jit(solution)/shard_map/all_gather | solution.py:278
  858.0 9.8 copy.292
  868.1 30.2 %all_gather.63 = bf16[8,16,3072]{2,1,0:T(8,128)(2,1)S(1)} all-gather(bf16[8,16,768]{2,1,0:T(8,128)(2,1)S(1)} %copy-done.72), channel_id=1, replica_groups=mesh['dp'=2,'row'=4,'col'=4] {'col'}, dimensions={2}, use_global_device_ids=true | all-gather | bytes 983040 | tf_op jit(solution)/shard_map/all_gather | solution.py:277
  928.8 11.8 fusion.137
  940.6 12.5 all-to-all-done.4
  975.9 41.4 %multiply_convert_fusion.1 = (bf16[1225,3072]{1,0:T(8,128)(2,1)}, f32[1225,3072]{1,0:T(8,128)}, f32[1225,3072]{1,0:T(8,128)}) fusion(f32[1225,3072]{1,0:T(8,128)S(1)} %fusion.135, f32[1225,16]{0,1:T(8,128)S(1)} %fusion.149, bf16[1,16,3072]{2,0,1:T(2,128)(2,1)S(1)} %fusion.64), kind=kOutput, calls=%fused_computation.9 | convolution fusion | flops 970905600 | bytes 52861504 | tf_op jit(solution)/shard_map/dot_general | solution.py:110
  1017.3 23.1 %add_convert_fusion = bf16[1225,3072]{1,0:T(8,128)(2,1)} fusion(f32[1225,3072]{1,0:T(8,128)} %get-tuple-element.32, f32[1225,3072]{1,0:T(8,128)} %fusion.137, f32[1225,3072]{1,0:T(8,128)} %get-tuple-element.51, f32[1225,16]{0,1:T(8,128)S(1)} %fusion.116, bf16[1,3072,16]{1,2,0:T(8,128)(2,1)S(1)} %copy.292), kind=kOutput, calls=%fused_computation.8 | convolution fusion | flops 778982400 | bytes 52861504 | tf_op jit(solution)/shard_map/dot_general | solution.py:117
  1062.8 26.9 %all_to_all.186 = bf16[1225,4,192]{0,2,1:T(8,128)(2,1)S(1)} all-to-all(bf16[1225,4,192]{0,2,1:T(8,128)(2,1)S(1)} %bitcast.307), channel_id=1, replica_groups=mesh['dp'=2,'row'=4,'col'=4] {'row'}, dimensions={1} | all-to-all | bytes 3763200 | tf_op jit(solution)/shard_map/all_to_all | solution.py:88
  1114.9 23.5 %all-to-all-done.8 = bf16[4,1225,192]{1,2,0:T(8,128)(2,1)S(1)} async-done(((bf16[4,1225,192]{1,2,0:T(8,128)(2,1)}), bf16[4,1225,192]{1,2,0:T(8,128)(2,1)S(1)}, u32[]{:S(2)}, u32[]{:S(2)}) %all-to-all-start.8) | async-done | bytes 1881632 | tf_op jit(solution)/shard_map/all_to_all | solution.py:94
  1154.1 9.9 fusion.136
  1187.7 9.3 reshape.212
  1197.0 11.3 convert_bitcast_fusion.5
  1208.2 21.7 %multiply_reduce_fusion = (f32[25,3,196]{2,1,0:T(4,128)S(1)}, f32[25,3,196,196]{2,3,1,0:T(8,128)}) fusion(f32[25,3,196,196]{2,3,1,0:T(8,128)} %get-tuple-element.50, f32[25,3,196]{2,1,0:T(4,128)S(1)} %log_add_fusion, bf16[25,196,3,1,64]{1,0,4,3,2:T(8,128)(2,1)} %get-tuple-element.35, bf16[25,196,3,64]{1,0,3,2:T(8,128)(2,1)S(1)} %reshape.212), kind=kOutput, calls=%fused_computation.2 | convolution fusion | flops 377422528 | bytes 26930400 | tf_op jit(solution)/shard_map/nqhc,nkhc->nhqk/dot_general | solution.py:185
  1230.0 11.2 multiply_convert_fusion
  1249.0 30.3 %copy.261 = f32[25,3,196,196]{0,3,2,1:T(8,128)} copy(bf16[25,3,196,196]{2,3,1,0:T(8,128)(2,1)} %copy-done.2) | data formatting | bytes 17287200 | tf_op jit(solution)/shard_map/reshape | solution.py:194
  1279.4 64.6 %reshape.221 = f32[25,3,14,14,14,14]{0,5,4,3,2,1:T(8,128)} reshape(f32[25,3,196,196]{0,3,2,1:T(8,128)} %copy.261) | data formatting | bytes 23049600 | tf_op jit(solution)/shard_map/reshape | solution.py:194
  1344.0 94.7 %fusion.128 = (f32[25,3,14,14,14]{0,4,3,2,1:T(8,128)}, f32[25,3,14,14,14]{0,4,3,2,1:T(8,128)}) fusion(f32[25,3,14,14,14,14]{0,5,4,3,2,1:T(8,128)} %reshape.221), kind=kLoop, calls=%fused_computation.231 | loop fusion | flops 5350800 | bytes 13171200 | tf_op jit(solution)/shard_map/reduce_sum | solution.py:195
  1438.7 10.2 fusion.14
  1464.8 8.9 reshape.215
  1494.7 11.8 copy.269
  1506.5 24.2 %convert_element_type.249 = bf16[4,1225,576]{1,0,2:T(4,128)(2,1)} reshape(bf16[25,196,3,3,64]{1,0,4,3,2:T(8,128)(2,1)} %copy.269) | data formatting | bytes 11289600 | tf_op jit(solution)/shard_map/convert_element_type | solution.py:205
  1577.8 31.0 %all-to-all-done.10 = bf16[4,1225,576]{1,2,0:T(8,128)(2,1)} async-done(((bf16[4,1225,576]{1,2,0:T(8,128)(2,1)}), bf16[4,1225,576]{1,2,0:T(8,128)(2,1)}, u32[]{:S(2)}, u32[]{:S(2)}) %all-to-all-start.10) | async-done | bytes 5644832 | tf_op jit(solution)/shard_map/all_to_all | solution.py:94
  1643.2 17.6 all-to-all-done.11
  1678.7 10.9 all-reduce.2
  1689.7 9.7 fusion.37
  1699.4 106.6 %all-reduce.6.cloned.1.call-done = (f32[8,768,16]{1,2,0:T(8,128)}, f32[8,16,2304]{2,1,0:T(8,128)}, f32[8,768,16]{1,2,0:T(8,128)}, f32[8,16,768]{2,1,0:T(8,128)},...) async-done(((f32[8,768,16]{1,2,0:T(8,128)}, f32[8,16,2304]{2,1,0:T(8,128)}, f32[8,768,16]{1,2,0:T(8,128)}, ...) | async-done | bytes 6291472 | tf_op jit(solution)/shard_map/psum | solution.py:326
  (370 shorter events, 457.7 us)
Async XLA Ops:
  7.2 354.6 %copy-start = (bf16[27,64]{1,0:T(8,128)(2,1)S(1)}, bf16[27,64]{1,0:T(8,128)(2,1)}, u32[]{:S(2)}) copy-start(bf16[27,64]{1,0:T(8,128)(2,1)} %param.28) | copy-start | bytes 10372
  7.2 12.9 copy-start.90
  7.2 12.9 copy-start.4
  7.2 225.9 %all-gather.7.cloned.1.call-start = ((), (), s32[]{:S(2)}) async-start(), calls=%async_computation.12 | async-start | bytes 4423680 | tf_op jit(solution)/shard_map/all_gather | solution.py:250
  20.1 14.9 copy-start.86
  41.5 191.2 %all-to-all-start = ((bf16[4,1225,192]{1,2,0:T(8,128)(2,1)}), bf16[4,1225,192]{1,2,0:T(8,128)(2,1)S(1)}, u32[]{:S(2)}, u32[]{:S(2)}) async-start(bf16[4,1225,192]{1,2,0:T(8,128)(2,1)} %copy.222), calls=%async_computation | async-start | bytes 3932160 | tf_op jit(solution)/shard_map/all_to_all | solution.py:94
  45.1 119.6 %copy-start.76 = (bf16[8,192,16]{1,2,0:T(8,128)(2,1)S(1)}, bf16[8,192,16]{1,2,0:T(8,128)(2,1)}, u32[]{:S(2)}) copy-start(bf16[8,192,16]{1,2,0:T(8,128)(2,1)} %param.34) | copy-start | bytes 147460
  45.1 317.2 %all-gather.15.cloned.1.call-start = ((), (), s32[]{:S(2)}) async-start(), calls=%async_computation.16 | async-start | bytes 1474560 | tf_op jit(solution)/shard_map/all_gather | solution.py:269
  45.9 119.1 %copy-start.77 = (bf16[8,192,16]{1,2,0:T(8,128)(2,1)S(1)}, bf16[8,192,16]{1,2,0:T(8,128)(2,1)}, u32[]{:S(2)}) copy-start(bf16[8,192,16]{1,2,0:T(8,128)(2,1)} %param.32) | copy-start | bytes 147460
  45.9 120.1 %copy-start.78 = (bf16[8,192,16]{1,2,0:T(8,128)(2,1)S(1)}, bf16[8,192,16]{1,2,0:T(8,128)(2,1)}, u32[]{:S(2)}) copy-start(bf16[8,192,16]{1,2,0:T(8,128)(2,1)} %param.30) | copy-start | bytes 147460
  171.6 56.4 %copy-start.91 = (s32[8,1]{0,1:T(1,128)S(1)}, s32[8,1]{0,1:T(1,128)}, u32[]{:S(2)}) copy-start(s32[8,1]{0,1:T(1,128)} %param.21) | copy-start | bytes 100
  228.7 11.7 copy-start.51
  256.5 81.9 %copy-start.79 = (bf16[8,16,192]{2,1,0:T(8,128)(2,1)S(1)}, bf16[8,16,192]{2,1,0:T(8,128)(2,1)}, u32[]{:S(2)}) copy-start(bf16[8,16,192]{2,1,0:T(8,128)(2,1)} %param.33) | copy-start | bytes 147460
  256.5 105.8 %all-to-all-start.1 = ((bf16[1225,4,576]{0,2,1:T(8,128)(2,1)}), bf16[1225,4,576]{0,2,1:T(8,128)(2,1)}, u32[]{:S(2)}, u32[]{:S(2)}) async-start(bf16[1225,4,576]{0,2,1:T(8,128)(2,1)} %bitcast.293), calls=%async_computation.1 | async-start | bytes 11796480 | tf_op jit(solution)/shard_map/all_to_all | solution.py:98
  261.8 91.5 %copy-start.93 = (u32[32]{0:T(128)S(1)}, u32[32]{0:T(128)}, u32[]{:S(2)}) copy-start(u32[32]{0:T(128)} %constant.173) | copy-start | bytes 388
  261.8 92.7 %copy-start.92 = (bf16[192]{0:T(256)(128)(2,1)S(1)}, bf16[192]{0:T(256)(128)(2,1)}, u32[]{:S(2)}) copy-start(bf16[192]{0:T(256)(128)(2,1)} %param.23) | copy-start | bytes 1156
  261.8 100.2 %copy-start.89 = (bf16[27,64]{1,0:T(8,128)(2,1)S(1)}, bf16[27,64]{1,0:T(8,128)(2,1)}, u32[]{:S(2)}) copy-start(bf16[27,64]{1,0:T(8,128)(2,1)} %param.29) | copy-start | bytes 10372
  261.9 572.0 %all-gather.11.cloned.1.call-start = ((), (), s32[]{:S(2)}) async-start(), calls=%async_computation.14 | async-start | bytes 1474560 | tf_op jit(solution)/shard_map/all_gather | solution.py:268
  262.6 571.3 %all-gather.9.cloned.1.call-start = ((), (), s32[]{:S(2)}) async-start(), calls=%async_computation.13 | async-start | bytes 1474560 | tf_op jit(solution)/shard_map/all_gather | solution.py:251
  338.4 590.4 %all-gather.17.cloned.1.call-start = ((), (), s32[]{:S(2)}) async-start(), calls=%async_computation.17 | async-start | bytes 5898240 | tf_op jit(solution)/shard_map/all_gather | solution.py:276
  362.0 190.1 %copy-start.63 = (bf16[14,14,64,1,1]{2,1,4,3,0:T(8,128)(2,1)}, bf16[14,14,64,1,1]{2,1,4,3,0:T(8,128)(2,1)S(1)}, u32[]{:S(2)}) copy-start(bf16[14,14,64,1,1]{2,1,4,3,0:T(8,128)(2,1)S(1)} %fusion.61) | copy-start | bytes 75268
  362.2 55.7 %copy-start.65 = (bf16[14,14,64]{2,1,0:T(8,128)(2,1)}, bf16[14,14,64]{2,1,0:T(8,128)(2,1)S(1)}, u32[]{:S(2)}) copy-start(bf16[14,14,64]{2,1,0:T(8,128)(2,1)S(1)} %convolution_convert_fusion) | copy-start | bytes 75268
  405.0 13.0 copy-start.8
  650.8 39.1 %copy-start.9 = (bf16[25,196,3,1,64]{1,0,4,3,2:T(8,128)(2,1)S(1)}, bf16[25,196,3,1,64]{1,0,4,3,2:T(8,128)(2,1)}, u32[]{:S(2)}) copy-start(bf16[25,196,3,1,64]{1,0,4,3,2:T(8,128)(2,1)} %copy-done.8) | copy-start | bytes 5644804
  746.5 27.9 %all-to-all-start.2 = ((bf16[4,1225,192]{1,2,0:T(8,128)(2,1)}), bf16[4,1225,192]{1,2,0:T(8,128)(2,1)S(1)}, u32[]{:S(2)}, u32[]{:S(2)}) async-start(bf16[4,1225,192]{1,2,0:T(8,128)(2,1)} %copy.240), calls=%async_computation.2 | async-start | bytes 3932160 | tf_op jit(solution)/shard_map/all_to_all | solution.py:94
  775.7 70.0 %all-to-all-start.6 = ((bf16[4,1225,192]{1,2,0:T(8,128)(2,1)}), bf16[4,1225,192]{1,2,0:T(8,128)(2,1)S(1)}, u32[]{:S(2)}, u32[]{:S(2)}) async-start(bf16[4,1225,192]{1,2,0:T(8,128)(2,1)} %copy.253), calls=%async_computation.6 | async-start | bytes 3932160 | tf_op jit(solution)/shard_map/all_to_all | solution.py:82
  779.3 188.6 %all-gather.13.cloned.1.call-start = ((), (), s32[]{:S(2)}) async-start(), calls=%async_computation.15 | async-start | bytes 5898240 | tf_op jit(solution)/shard_map/all_gather | solution.py:275
  845.7 53.3 %copy-start.11 = (bf16[4,1225,192]{1,2,0:T(8,128)(2,1)}, bf16[4,1225,192]{1,2,0:T(8,128)(2,1)S(1)}, u32[]{:S(2)}) copy-start(bf16[4,1225,192]{1,2,0:T(8,128)(2,1)S(1)} %all-to-all-done.6) | copy-start | bytes 5644804
  845.7 53.6 %all-to-all-start.3 = ((bf16[1225,4,192]{0,2,1:T(8,128)(2,1)}), bf16[1225,4,192]{0,2,1:T(8,128)(2,1)}, u32[]{:S(2)}, u32[]{:S(2)}) async-start(bf16[1225,4,192]{0,2,1:T(8,128)(2,1)} %bitcast.305), calls=%async_computation.3 | async-start | bytes 3932160 | tf_op jit(solution)/shard_map/all_to_all | solution.py:102
  867.8 149.5 %copy-start.55 = (bf16[1,3072,16]{1,2,0:T(8,128)(2,1)}, bf16[1,3072,16]{1,2,0:T(8,128)(2,1)S(1)}, u32[]{:S(2)}) copy-start(bf16[1,3072,16]{1,2,0:T(8,128)(2,1)S(1)} %copy.292) | copy-start | bytes 294916
  868.1 30.9 %copy-start.69 = (bf16[1,16,768]{2,0,1:T(2,128)(2,1)}, bf16[1,16,768]{2,0,1:T(2,128)(2,1)S(1)}, u32[]{:S(2)}) copy-start(bf16[1,16,768]{2,0,1:T(2,128)(2,1)S(1)} %fusion.119) | copy-start | bytes 73732
  899.3 118.0 %copy-start.61 = (f32[1225,16]{0,1:T(8,128)}, f32[1225,16]{0,1:T(8,128)S(1)}, u32[]{:S(2)}) copy-start(f32[1225,16]{0,1:T(8,128)S(1)} %fusion.116) | copy-start | bytes 235204
  924.1 29.0 %all-to-all-start.4 = ((bf16[4,1225,192]{1,2,0:T(8,128)(2,1)}), bf16[4,1225,192]{1,2,0:T(8,128)(2,1)}, u32[]{:S(2)}, u32[]{:S(2)}) async-start(bf16[4,1225,192]{1,2,0:T(8,128)(2,1)} %copy.247), calls=%async_computation.4 | async-start | bytes 3932160 | tf_op jit(solution)/shard_map/all_to_all | solution.py:82
  1109.1 29.3 %copy-start.68 = (bf16[1,16,768]{2,0,1:T(2,128)(2,1)S(1)}, bf16[1,16,768]{2,0,1:T(2,128)(2,1)}, u32[]{:S(2)}) copy-start(bf16[1,16,768]{2,0,1:T(2,128)(2,1)} %fusion.123) | copy-start | bytes 73732
  1110.5 27.9 %all-to-all-start.8 = ((bf16[4,1225,192]{1,2,0:T(8,128)(2,1)}), bf16[4,1225,192]{1,2,0:T(8,128)(2,1)S(1)}, u32[]{:S(2)}, u32[]{:S(2)}) async-start(bf16[4,1225,192]{1,2,0:T(8,128)(2,1)} %copy.256), calls=%async_computation.8 | async-start | bytes 3932160 | tf_op jit(solution)/shard_map/all_to_all | solution.py:94
  1149.2 14.9 slice-start
  1149.2 29.3 %all-to-all-start.9 = ((bf16[1225,4,192]{0,2,1:T(8,128)(2,1)}), bf16[1225,4,192]{0,2,1:T(8,128)(2,1)}, u32[]{:S(2)}, u32[]{:S(2)}) async-start(bf16[1225,4,192]{0,2,1:T(8,128)(2,1)} %bitcast.306), calls=%async_computation.9 | async-start | bytes 3932160 | tf_op jit(solution)/shard_map/all_to_all | solution.py:98
  1178.5 358.2 %all-to-all-start.5 = ((bf16[1225,4,192]{0,2,1:T(8,128)(2,1)}), bf16[1225,4,192]{0,2,1:T(8,128)(2,1)}, u32[]{:S(2)}, u32[]{:S(2)}) async-start(bf16[1225,4,192]{0,2,1:T(8,128)(2,1)} %bitcast.38), calls=%async_computation.5 | async-start | bytes 3932160 | tf_op jit(solution)/shard_map/all_to_all | solution.py:88
  1230.0 14.2 copy-start.10
  1343.9 94.8 %copy-start.66 = (bf16[14,14,64]{2,1,0:T(8,128)(2,1)S(1)}, bf16[14,14,64]{2,1,0:T(8,128)(2,1)}, u32[]{:S(2)}) copy-start(bf16[14,14,64]{2,1,0:T(8,128)(2,1)} %copy-done.65) | copy-start | bytes 75268
  1438.7 10.3 copy-start.14
  1438.7 10.3 copy-start.64
  1536.7 17.4 slice-start.2
  1536.7 72.1 %all-to-all-start.10 = ((bf16[4,1225,576]{1,2,0:T(8,128)(2,1)}), bf16[4,1225,576]{1,2,0:T(8,128)(2,1)}, u32[]{:S(2)}, u32[]{:S(2)}) async-start(bf16[4,1225,576]{1,2,0:T(8,128)(2,1)} %copy.270), calls=%async_computation.10 | async-start | bytes 11796480 | tf_op jit(solution)/shard_map/all_to_all | solution.py:94
  1571.9 37.0 %copy-start.52 = (bf16[1,16,2304]{2,0,1:T(2,128)(2,1)S(1)}, bf16[1,16,2304]{2,0,1:T(2,128)(2,1)}, u32[]{:S(2)}) copy-start(bf16[1,16,2304]{2,0,1:T(2,128)(2,1)} %copy-done.51) | copy-start | bytes 221188
  1627.2 33.6 %all-to-all-start.11 = ((bf16[1225,4,192]{0,2,1:T(8,128)(2,1)}), bf16[1225,4,192]{0,2,1:T(8,128)(2,1)}, u32[]{:S(2)}, u32[]{:S(2)}) async-start(bf16[1225,4,192]{0,2,1:T(8,128)(2,1)} %bitcast.304), calls=%async_computation.11 | async-start | bytes 3932160 | tf_op jit(solution)/shard_map/all_to_all | solution.py:102
  1631.8 174.2 %all-reduce.6.cloned.1.call-start = ((), (), s32[]{:S(2)}) async-start(), calls=%async_computation.18 | async-start | bytes 12582912 | tf_op jit(solution)/shard_map/psum | solution.py:326
  1689.6 130.2 %copy-start.1 = (bf16[27,64]{1,0:T(8,128)(2,1)S(1)}, bf16[27,64]{1,0:T(8,128)(2,1)}, u32[]{:S(2)}) copy-start(bf16[27,64]{1,0:T(8,128)(2,1)} %param.28) | copy-start | bytes 10372
  (68 other events, 430.7 us)
Sparse Core Ops, SparseCore 0:
  20.2 108.6 all-gather.6
  130.5 16.0 all-gather.14
  264.3 24.6 all-gather.10
  338.5 29.8 all-gather.8
  369.8 88.5 all-gather.16
  834.0 100.3 all-gather.12
  1643.3 162.6 all-reduce.5
where the time goes:
time: 1840 us; the launch traced here: 1830 us
  local copies, waits for them, and re-layouts  647 us (35%)
  blocking collectives  412 us (22%)
  matrix products  314 us (17%)
  waiting for transfers between devices  211 us (11%)
  other arithmetic  177 us (10%)
  starting transfers between devices  49.4 us (3%)
    add x6, local copies, waits for them, and re-layouts, score_matrix(): shaped + rel_rows[:, :, :, :, :, None] + rel_cols[:, :, :, :, None, :]  251 us
    all_gather x1, blocking collectives, body(): lax.all_gather(qkv_up, 'col', axis=2, tiled=True)  118 us
    psum x1, waiting for transfers between devices, body(): lax.psum((spread_pick(own_pick, qkv_pair[0]), spread_pick(own_pick, qkv_p...  107 us
    reshape x2, local copies, waits for them, and re-layouts, attend_back(): grad_s.astype(jnp.float32).reshape(windows, heads_local, WIN, WIN, WIN, WIN)  94.9 us
    reduce_sum x1, other arithmetic, attend_back(): along_rows = jnp.sum(split_grad, axis=5)  94.7 us
    all_gather x1, blocking collectives, body(): lax.all_gather(proj_weight, 'row', axis=1, tiled=True)  74.5 us
    all_to_all x4, waiting for transfers between devices, token_rows(): lax.all_to_all(values, 'row', split_axis=0, concat_axis=1, tiled=True)  65.1 us
    dot_general x4, matrix products, adapted_local(): jnp.dot(reduced, up_mat.astype(jnp.float32), precision=PRECISE)  53.4 us
  transfers between devices with their start and end apart: 18, of which 7 were waited for; matrix products, arithmetic and copies ran while one was open for 52% of the time, Pallas kernels for 0%

commit v1 on v0

--- a/solution.py
+++ b/solution.py
@@ -12,6 +12,19 @@
 IMG_TOK = 4900
 PRECISE = lax.Precision.HIGHEST
 EPSILON = 1e-06
+
+
+def gather_around(value, axis, dim):
+    ways = lax.axis_size(axis)
+    up = [(d, (d + 1) % ways) for d in range(ways)]
+    down = [(d, (d - 1) % ways) for d in range(ways)]
+    earlier, later = ([value], [value])
+    for _ in range(ways // 2):
+        earlier.append(lax.ppermute(earlier[-1], axis, up))
+    for _ in range((ways - 1) // 2):
+        later.append(lax.ppermute(later[-1], axis, down))
+    line = jnp.concatenate([*earlier[::-1], *later[1:]], axis=dim)
+    return jnp.roll(line, (lax.axis_index(axis) - ways // 2) * value.shape[dim], axis=dim)
 
 
 def exact_gelu(values):
@@ -249,7 +262,7 @@
     qkv_full, proj_full, qkv_up_all, proj_dn_all = (
         lax.all_gather(qkv_part, "col", axis=1, tiled=True),
         lax.all_gather(proj_part, "col", axis=0, tiled=True),
-        lax.all_gather(qkv_up, "col", axis=2, tiled=True),
+        gather_around(qkv_up, "col", 2),
         lax.all_gather(proj_down, "col", axis=1, tiled=True),
     )
     qkv_dn = pick_one(qkv_dn_part, own_pick)

time: 1840 us -> 1760 us (0.957)
  blocking collectives: 412 us -> 317 us
    all_gather x1 -> x0, blocking collectives: 118 us -> none  [body(): lax.all_gather(qkv_up, 'col', axis=2, tiled=True)]
    all_gather x1, blocking collectives: 12.9 us -> 31.9 us  [body(): lax.all_gather(fc1_down, 'row', axis=1, tiled=True)]
  transfers between devices with their start and end apart: 18 -> 21, of which waited for: 7 -> 8; matrix products, arithmetic and copies ran while one was open for 52% -> 55% of each run, Pallas kernels for 0% -> 0%
where the time goes in v1:
time: 1760 us; the launch traced here: 1740 us
  local copies, waits for them, and re-layouts  647 us (37%)
  blocking collectives  317 us (18%)
  matrix products  314 us (18%)
  waiting for transfers between devices  213 us (12%)
  other arithmetic  179 us (10%)
  starting transfers between devices  54 us (3%)
    add x6, local copies, waits for them, and re-layouts, score_matrix(): shaped + rel_rows[:, :, :, :, :, None] + rel_cols[:, :, :, :, None, :]  251 us
    psum x1, waiting for transfers between devices, body(): lax.psum((spread_pick(own_pick, qkv_pair[0]), spread_pick(own_pick, qkv_p...  107 us
    reshape x2, local copies, waits for them, and re-layouts, attend_back(): grad_s.astype(jnp.float32).reshape(windows, heads_local, WIN, WIN, WIN, WIN)  94.9 us
    reduce_sum x1, other arithmetic, attend_back(): along_rows = jnp.sum(split_grad, axis=5)  94.7 us
    all_gather x1, blocking collectives, body(): lax.all_gather(proj_weight, 'row', axis=1, tiled=True)  74.7 us
    all_to_all x4, waiting for transfers between devices, token_rows(): lax.all_to_all(values, 'row', split_axis=0, concat_axis=1, tiled=True)  65.1 us
    dot_general x4, matrix products, adapted_local(): jnp.dot(reduced, up_mat.astype(jnp.float32), precision=PRECISE)  53.4 us
  transfers between devices with their start and end apart: 21, of which 8 were waited for; matrix products, arithmetic and copies ran while one was open for 55% of the time, Pallas kernels for 0%

profile of v1, /device:TPU:0, one launch (start us, length us, event | category | flops | bytes accessed | tf_op | source)
XLA Modules:
  0.0 1740.0 jit_solution(5098488279250587304)
XLA Ops:
  7.3 11.5 all_gather.48
  24.7 11.9 all-reduce.3
  51.2 31.9 %all_gather.58 = bf16[8,768,16]{2,0,1:T(8,128)(2,1)S(1)} all-gather(bf16[8,192,16]{2,0,1:T(8,128)(2,1)} %copy.246), channel_id=1, replica_groups=mesh['dp'=2,'row'=4,'col'=4] {'row'}, dimensions={1}, use_global_device_ids=true | all-gather | bytes 245760 | tf_op jit(solution)/shard_map/all_gather | solution.py:283
  84.9 32.4 %all_gather.53 = bf16[8,768,16]{2,0,1:T(8,128)(2,1)} all-gather(bf16[8,192,16]{2,0,1:T(8,128)(2,1)} %copy.240), channel_id=1, replica_groups=mesh['dp'=2,'row'=4,'col'=4] {'col'}, dimensions={1}, use_global_device_ids=true | all-gather | bytes 245760 | tf_op jit(solution)/shard_map/all_gather | solution.py:266
  119.2 15.7 all_gather.50
  161.8 8.9 copy.223
  177.1 74.7 %all_gather.51 = bf16[192,768]{0,1:T(8,128)(2,1)S(1)} all-gather(bf16[192,192]{0,1:T(8,128)(2,1)S(1)} %copy.238), channel_id=1, replica_groups=mesh['dp'=2,'row'=4,'col'=4] {'row'}, dimensions={1}, use_global_device_ids=true | all-gather | bytes 368640 | tf_op jit(solution)/shard_map/all_gather | solution.py:258
  253.0 13.0 all_gather.54
  276.7 9.7 copy.224
  286.4 26.8 %reshape.211 = bf16[25,196,3,3,64]{1,0,4,3,2:T(8,128)(2,1)} reshape(bf16[4,1225,576]{1,0,2:T(4,128)(2,1)} %copy.224) | data formatting | bytes 11289600 | tf_op jit(solution)/shard_map/reshape | solution.py:155
  341.5 21.4 %add.284 = f32[25,3,14,14,14,14]{0,5,4,3,2,1:T(8,128)} broadcast(f32[25,3,14,14,14]{0,4,3,2,1:T(8,128)S(1)} %copy.233), dimensions={0,1,2,3,5} | broadcast | bytes 12348000 | tf_op jit(solution)/shard_map/add | solution.py:173
  362.9 64.5 %add.285 = f32[25,3,196,196]{0,3,2,1:T(8,128)} reshape(f32[25,3,14,14,14,14]{0,5,4,3,2,1:T(8,128)} %add.284) | data formatting | bytes 23049600 | tf_op jit(solution)/shard_map/add | solution.py:173
  427.4 39.1 %copy.234 = f32[25,3,196,196]{2,3,1,0:T(8,128)} copy(f32[25,3,196,196]{0,3,2,1:T(8,128)} %add.285) | data formatting | bytes 23049600 | tf_op jit(solution)/shard_map/add | solution.py:173
  477.8 22.8 %add.281 = f32[25,3,14,14,14,14]{0,5,4,3,2,1:T(8,128)} broadcast(f32[25,3,14,14,14]{0,4,3,2,1:T(8,128)} %copy.230), dimensions={0,1,2,3,4} | broadcast | bytes 12348000 | tf_op jit(solution)/shard_map/add | solution.py:173
  500.6 64.5 %add.282 = f32[25,3,196,196]{0,3,2,1:T(8,128)} reshape(f32[25,3,14,14,14,14]{0,5,4,3,2,1:T(8,128)} %add.281) | data formatting | bytes 23049600 | tf_op jit(solution)/shard_map/add | solution.py:173
  565.1 39.1 %copy.231 = f32[25,3,196,196]{2,3,1,0:T(8,128)} copy(f32[25,3,196,196]{0,3,2,1:T(8,128)} %add.282) | data formatting | bytes 23049600 | tf_op jit(solution)/shard_map/add | solution.py:173
  604.2 24.5 %fusion.133 = (f32[25,3,196]{2,1,0:T(4,128)S(1)}, f32[25,3,196,196]{2,3,1,0:T(8,128)}) fusion(f32[25,3,196,196]{2,3,1,0:T(8,128)} %copy.234, f32[25,3,196,196]{2,3,1,0:T(8,128)} %copy.231, bf16[25,196,3,1,64]{1,0,4,3,2:T(8,128)(2,1)} %get-tuple-element.37, bf16[25,196,3,1,64]{1,0,4,3,2:T(8,128)(2,1)S(1)} %copy-done.9), kind=kOutput, calls=%fused_computation.236 | convolution fusion | flops 380303744 | bytes 38396400 | tf_op jit(solution)/shard_map/nqhc,nkhc->nhqk/dot_general | solution.py:162
  628.8 9.8 fusion.6
  638.6 10.1 convert_bitcast_fusion.6
  678.1 10.6 all-to-all-done.2
  693.7 33.6 %all_gather.63 = bf16[8,16,768]{1,0,2:T(8,128)(2,1)S(1)} all-gather(bf16[8,16,192]{1,0,2:T(8,128)(2,1)} %copy.247), channel_id=1, replica_groups=mesh['dp'=2,'row'=4,'col'=4] {'row'}, dimensions={2}, use_global_device_ids=true | all-gather | bytes 245760 | tf_op jit(solution)/shard_map/all_gather | solution.py:284
  728.9 18.1 %all_gather.62 = bf16[8,3072,16]{1,2,0:T(8,128)(2,1)S(1)} all-gather(bf16[8,768,16]{1,2,0:T(8,128)(2,1)} %param.36), channel_id=1, replica_groups=mesh['dp'=2,'row'=4,'col'=4] {'col'}, dimensions={1}, use_global_device_ids=true | all-gather | bytes 983040 | tf_op jit(solution)/shard_map/all_gather | solution.py:291
  771.2 9.8 copy.289
  781.2 30.2 %all_gather.59 = bf16[8,16,3072]{2,1,0:T(8,128)(2,1)S(1)} all-gather(bf16[8,16,768]{2,1,0:T(8,128)(2,1)S(1)} %copy-done.72), channel_id=1, replica_groups=mesh['dp'=2,'row'=4,'col'=4] {'col'}, dimensions={2}, use_global_device_ids=true | all-gather | bytes 983040 | tf_op jit(solution)/shard_map/all_gather | solution.py:290
  841.9 11.8 fusion.138
  853.8 12.5 all-to-all-done.4
  889.1 41.4 %multiply_convert_fusion.1 = (bf16[1225,3072]{1,0:T(8,128)(2,1)}, f32[1225,3072]{1,0:T(8,128)}, f32[1225,3072]{1,0:T(8,128)}) fusion(f32[1225,3072]{1,0:T(8,128)S(1)} %fusion.136, f32[1225,16]{0,1:T(8,128)S(1)} %fusion.150, bf16[1,16,3072]{2,0,1:T(2,128)(2,1)S(1)} %fusion.64), kind=kOutput, calls=%fused_computation.9 | convolution fusion | flops 970905600 | bytes 52861504 | tf_op jit(solution)/shard_map/dot_general | solution.py:123
  930.5 23.1 %add_convert_fusion = bf16[1225,3072]{1,0:T(8,128)(2,1)} fusion(f32[1225,3072]{1,0:T(8,128)} %get-tuple-element.32, f32[1225,3072]{1,0:T(8,128)} %fusion.138, f32[1225,3072]{1,0:T(8,128)} %get-tuple-element.51, f32[1225,16]{0,1:T(8,128)S(1)} %fusion.118, bf16[1,3072,16]{1,2,0:T(8,128)(2,1)S(1)} %copy.289), kind=kOutput, calls=%fused_computation.8 | convolution fusion | flops 778982400 | bytes 52861504 | tf_op jit(solution)/shard_map/dot_general | solution.py:130
  958.9 8.7 fusion.139
  975.9 26.9 %all_to_all.186 = bf16[1225,4,192]{0,2,1:T(8,128)(2,1)S(1)} all-to-all(bf16[1225,4,192]{0,2,1:T(8,128)(2,1)S(1)} %bitcast.306), channel_id=1, replica_groups=mesh['dp'=2,'row'=4,'col'=4] {'row'}, dimensions={1} | all-to-all | bytes 3763200 | tf_op jit(solution)/shard_map/all_to_all | solution.py:101
  1028.1 23.5 %all-to-all-done.8 = bf16[4,1225,192]{1,2,0:T(8,128)(2,1)S(1)} async-done(((bf16[4,1225,192]{1,2,0:T(8,128)(2,1)}), bf16[4,1225,192]{1,2,0:T(8,128)(2,1)S(1)}, u32[]{:S(2)}, u32[]{:S(2)}) %all-to-all-start.8) | async-done | bytes 1881632 | tf_op jit(solution)/shard_map/all_to_all | solution.py:107
  1067.3 9.9 fusion.137
  1100.8 9.3 reshape.212
  1110.1 11.3 convert_bitcast_fusion.5
  1121.4 21.7 %multiply_reduce_fusion = (f32[25,3,196]{2,1,0:T(4,128)S(1)}, f32[25,3,196,196]{2,3,1,0:T(8,128)}) fusion(f32[25,3,196,196]{2,3,1,0:T(8,128)} %get-tuple-element.50, f32[25,3,196]{2,1,0:T(4,128)S(1)} %log_add_fusion, bf16[25,196,3,1,64]{1,0,4,3,2:T(8,128)(2,1)} %get-tuple-element.35, bf16[25,196,3,64]{1,0,3,2:T(8,128)(2,1)S(1)} %reshape.212), kind=kOutput, calls=%fused_computation.2 | convolution fusion | flops 377422528 | bytes 26930400 | tf_op jit(solution)/shard_map/nqhc,nkhc->nhqk/dot_general | solution.py:198
  1143.1 11.2 multiply_convert_fusion
  1162.2 30.3 %copy.258 = f32[25,3,196,196]{0,3,2,1:T(8,128)} copy(bf16[25,3,196,196]{2,3,1,0:T(8,128)(2,1)} %copy-done.2) | data formatting | bytes 17287200 | tf_op jit(solution)/shard_map/reshape | solution.py:207
  1192.5 64.6 %reshape.221 = f32[25,3,14,14,14,14]{0,5,4,3,2,1:T(8,128)} reshape(f32[25,3,196,196]{0,3,2,1:T(8,128)} %copy.258) | data formatting | bytes 23049600 | tf_op jit(solution)/shard_map/reshape | solution.py:207
  1257.1 94.7 %fusion.129 = (f32[25,3,14,14,14]{0,4,3,2,1:T(8,128)}, f32[25,3,14,14,14]{0,4,3,2,1:T(8,128)}) fusion(f32[25,3,14,14,14,14]{0,5,4,3,2,1:T(8,128)} %reshape.221), kind=kLoop, calls=%fused_computation.233 | loop fusion | flops 5350800 | bytes 13171200 | tf_op jit(solution)/shard_map/reduce_sum | solution.py:208
  1351.8 10.2 fusion.14
  1377.9 8.9 reshape.215
  1407.8 11.8 copy.266
  1419.7 24.2 %convert_element_type.249 = bf16[4,1225,576]{1,0,2:T(4,128)(2,1)} reshape(bf16[25,196,3,3,64]{1,0,4,3,2:T(8,128)(2,1)} %copy.266) | data formatting | bytes 11289600 | tf_op jit(solution)/shard_map/convert_element_type | solution.py:218
  1490.9 31.0 %all-to-all-done.10 = bf16[4,1225,576]{1,2,0:T(8,128)(2,1)} async-done(((bf16[4,1225,576]{1,2,0:T(8,128)(2,1)}), bf16[4,1225,576]{1,2,0:T(8,128)(2,1)}, u32[]{:S(2)}, u32[]{:S(2)}) %all-to-all-start.10) | async-done | bytes 5644832 | tf_op jit(solution)/shard_map/all_to_all | solution.py:107
  1556.4 17.6 %all-to-all-done.11 = bf16[1225,4,192]{0,2,1:T(8,128)(2,1)} async-done(((bf16[1225,4,192]{0,2,1:T(8,128)(2,1)}), bf16[1225,4,192]{0,2,1:T(8,128)(2,1)}, u32[]{:S(2)}, u32[]{:S(2)}) %all-to-all-start.11) | async-done | bytes 1881632 | tf_op jit(solution)/shard_map/all_to_all | solution.py:115
  1591.8 10.9 all-reduce.2
  1602.8 9.7 fusion.37
  1612.5 106.7 %all-reduce.6.cloned.1.call-done = (f32[8,768,16]{1,2,0:T(8,128)}, f32[8,16,2304]{2,1,0:T(8,128)}, f32[8,768,16]{1,2,0:T(8,128)}, f32[8,16,768]{2,1,0:T(8,128)},...) async-done(((f32[8,768,16]{1,2,0:T(8,128)}, f32[8,16,2304]{2,1,0:T(8,128)}, f32[8,768,16]{1,2,0:T(8,128)}, ...) | async-done | bytes 6291472 | tf_op jit(solution)/shard_map/psum | solution.py:339
  (369 shorter events, 457.2 us)
Async XLA Ops:
  7.2 269.0 %copy-start = (bf16[27,64]{1,0:T(8,128)(2,1)S(1)}, bf16[27,64]{1,0:T(8,128)(2,1)}, u32[]{:S(2)}) copy-start(bf16[27,64]{1,0:T(8,128)(2,1)} %param.28) | copy-start | bytes 10372
  7.2 16.8 copy-start.87
  7.2 16.8 copy-start.4
  7.2 140.1 %all-gather.7.cloned.1.call-start = ((), (), s32[]{:S(2)}) async-start(), calls=%async_computation.12 | async-start | bytes 4423680 | tf_op jit(solution)/shard_map/all_gather | solution.py:263
  20.1 114.9 %collective-permute-start = (bf16[8,16,576]{2,1,0:T(8,128)(2,1)}, bf16[8,16,576]{2,1,0:T(8,128)(2,1)}, u32[]{:S(2)}, u32[]{:S(2)}) collective-permute-start(bf16[8,16,576]{2,1,0:T(8,128)(2,1)} %param.31), channel_id=1, source_target_pairs={{0,1},{1,2},{2,3},{3,0},{4,5},{5,6},{6,7},{7,4},{8,9},{9,10},{10,1... | collective-permute-start | bytes 442376 | tf_op jit(solution)/shard_map/ppermute | solution.py:23
  21.7 119.8 %collective-permute-start.2 = (bf16[8,16,576]{2,1,0:T(8,128)(2,1)}, bf16[8,16,576]{2,1,0:T(8,128)(2,1)}, u32[]{:S(2)}, u32[]{:S(2)}) collective-permute-start(bf16[8,16,576]{2,1,0:T(8,128)(2,1)} %param.31), channel_id=1, source_target_pairs={{0,3},{1,0},{2,1},{3,2},{4,7},{5,4},{6,5},{7,6},{8,11},{9,8},{10,9... | collective-permute-start | bytes 442376 | tf_op jit(solution)/shard_map/ppermute | solution.py:25
  24.0 15.3 copy-start.83
  45.7 73.3 %copy-start.88 = (s32[8,1]{0,1:T(1,128)S(1)}, s32[8,1]{0,1:T(1,128)}, u32[]{:S(2)}) copy-start(s32[8,1]{0,1:T(1,128)} %param.21) | copy-start | bytes 100
  45.7 101.1 %all-to-all-start = ((bf16[4,1225,192]{1,2,0:T(8,128)(2,1)}), bf16[4,1225,192]{1,2,0:T(8,128)(2,1)S(1)}, u32[]{:S(2)}, u32[]{:S(2)}) async-start(bf16[4,1225,192]{1,2,0:T(8,128)(2,1)} %copy.220), calls=%async_computation | async-start | bytes 3932160 | tf_op jit(solution)/shard_map/all_to_all | solution.py:107
  49.5 227.2 %all-gather.15.cloned.1.call-start = ((), (), s32[]{:S(2)}) async-start(), calls=%async_computation.16 | async-start | bytes 1474560 | tf_op jit(solution)/shard_map/all_gather | solution.py:282
  135.0 11.5 copy-start.81
  135.0 8.8 collective-permute-start.1
  170.6 82.1 %copy-start.76 = (bf16[8,16,192]{2,1,0:T(8,128)(2,1)S(1)}, bf16[8,16,192]{2,1,0:T(8,128)(2,1)}, u32[]{:S(2)}) copy-start(bf16[8,16,192]{2,1,0:T(8,128)(2,1)} %param.33) | copy-start | bytes 147460
  170.6 106.0 %all-to-all-start.1 = ((bf16[1225,4,576]{0,2,1:T(8,128)(2,1)}), bf16[1225,4,576]{0,2,1:T(8,128)(2,1)}, u32[]{:S(2)}, u32[]{:S(2)}) async-start(bf16[1225,4,576]{0,2,1:T(8,128)(2,1)} %bitcast.292), calls=%async_computation.1 | async-start | bytes 11796480 | tf_op jit(solution)/shard_map/all_to_all | solution.py:111
  176.2 91.5 %copy-start.90 = (u32[32]{0:T(128)S(1)}, u32[32]{0:T(128)}, u32[]{:S(2)}) copy-start(u32[32]{0:T(128)} %constant.193) | copy-start | bytes 388
  176.2 92.7 %copy-start.89 = (bf16[192]{0:T(256)(128)(2,1)S(1)}, bf16[192]{0:T(256)(128)(2,1)}, u32[]{:S(2)}) copy-start(bf16[192]{0:T(256)(128)(2,1)} %param.23) | copy-start | bytes 1156
  176.2 100.2 %copy-start.86 = (bf16[27,64]{1,0:T(8,128)(2,1)S(1)}, bf16[27,64]{1,0:T(8,128)(2,1)}, u32[]{:S(2)}) copy-start(bf16[27,64]{1,0:T(8,128)(2,1)} %param.29) | copy-start | bytes 10372
  176.2 570.8 %all-gather.11.cloned.1.call-start = ((), (), s32[]{:S(2)}) async-start(), calls=%async_computation.14 | async-start | bytes 1474560 | tf_op jit(solution)/shard_map/all_gather | solution.py:281
  176.9 570.1 %all-gather.9.cloned.1.call-start = ((), (), s32[]{:S(2)}) async-start(), calls=%async_computation.13 | async-start | bytes 1474560 | tf_op jit(solution)/shard_map/all_gather | solution.py:264
  252.7 589.2 %all-gather.17.cloned.1.call-start = ((), (), s32[]{:S(2)}) async-start(), calls=%async_computation.17 | async-start | bytes 5898240 | tf_op jit(solution)/shard_map/all_gather | solution.py:289
  276.4 190.1 %copy-start.63 = (bf16[14,14,64,1,1]{2,1,4,3,0:T(8,128)(2,1)}, bf16[14,14,64,1,1]{2,1,4,3,0:T(8,128)(2,1)S(1)}, u32[]{:S(2)}) copy-start(bf16[14,14,64,1,1]{2,1,4,3,0:T(8,128)(2,1)S(1)} %fusion.61) | copy-start | bytes 75268
  276.6 55.7 %copy-start.65 = (bf16[14,14,64]{2,1,0:T(8,128)(2,1)}, bf16[14,14,64]{2,1,0:T(8,128)(2,1)S(1)}, u32[]{:S(2)}) copy-start(bf16[14,14,64]{2,1,0:T(8,128)(2,1)S(1)} %convolution_convert_fusion) | copy-start | bytes 75268
  319.4 13.0 copy-start.8
  565.1 39.1 %copy-start.9 = (bf16[25,196,3,1,64]{1,0,4,3,2:T(8,128)(2,1)S(1)}, bf16[25,196,3,1,64]{1,0,4,3,2:T(8,128)(2,1)}, u32[]{:S(2)}) copy-start(bf16[25,196,3,1,64]{1,0,4,3,2:T(8,128)(2,1)} %copy-done.8) | copy-start | bytes 5644804
  660.8 27.9 %all-to-all-start.2 = ((bf16[4,1225,192]{1,2,0:T(8,128)(2,1)}), bf16[4,1225,192]{1,2,0:T(8,128)(2,1)S(1)}, u32[]{:S(2)}, u32[]{:S(2)}) async-start(bf16[4,1225,192]{1,2,0:T(8,128)(2,1)} %copy.237), calls=%async_computation.2 | async-start | bytes 3932160 | tf_op jit(solution)/shard_map/all_to_all | solution.py:107
  690.0 68.8 %all-to-all-start.6 = ((bf16[4,1225,192]{1,2,0:T(8,128)(2,1)}), bf16[4,1225,192]{1,2,0:T(8,128)(2,1)S(1)}, u32[]{:S(2)}, u32[]{:S(2)}) async-start(bf16[4,1225,192]{1,2,0:T(8,128)(2,1)} %copy.250), calls=%async_computation.6 | async-start | bytes 3932160 | tf_op jit(solution)/shard_map/all_to_all | solution.py:95
  693.6 187.4 %all-gather.13.cloned.1.call-start = ((), (), s32[]{:S(2)}) async-start(), calls=%async_computation.15 | async-start | bytes 5898240 | tf_op jit(solution)/shard_map/all_gather | solution.py:288
  758.8 53.2 %copy-start.11 = (bf16[4,1225,192]{1,2,0:T(8,128)(2,1)}, bf16[4,1225,192]{1,2,0:T(8,128)(2,1)S(1)}, u32[]{:S(2)}) copy-start(bf16[4,1225,192]{1,2,0:T(8,128)(2,1)S(1)} %all-to-all-done.6) | copy-start | bytes 5644804
  758.8 53.6 %all-to-all-start.3 = ((bf16[1225,4,192]{0,2,1:T(8,128)(2,1)}), bf16[1225,4,192]{0,2,1:T(8,128)(2,1)}, u32[]{:S(2)}, u32[]{:S(2)}) async-start(bf16[1225,4,192]{0,2,1:T(8,128)(2,1)} %bitcast.304), calls=%async_computation.3 | async-start | bytes 3932160 | tf_op jit(solution)/shard_map/all_to_all | solution.py:115
  781.0 149.5 %copy-start.55 = (bf16[1,3072,16]{1,2,0:T(8,128)(2,1)}, bf16[1,3072,16]{1,2,0:T(8,128)(2,1)S(1)}, u32[]{:S(2)}) copy-start(bf16[1,3072,16]{1,2,0:T(8,128)(2,1)S(1)} %copy.289) | copy-start | bytes 294916
  781.2 30.9 %copy-start.69 = (bf16[1,16,768]{2,0,1:T(2,128)(2,1)}, bf16[1,16,768]{2,0,1:T(2,128)(2,1)S(1)}, u32[]{:S(2)}) copy-start(bf16[1,16,768]{2,0,1:T(2,128)(2,1)S(1)} %fusion.121) | copy-start | bytes 73732
  812.4 118.0 %copy-start.61 = (f32[1225,16]{0,1:T(8,128)}, f32[1225,16]{0,1:T(8,128)S(1)}, u32[]{:S(2)}) copy-start(f32[1225,16]{0,1:T(8,128)S(1)} %fusion.118) | copy-start | bytes 235204
  837.2 29.0 %all-to-all-start.4 = ((bf16[4,1225,192]{1,2,0:T(8,128)(2,1)}), bf16[4,1225,192]{1,2,0:T(8,128)(2,1)}, u32[]{:S(2)}, u32[]{:S(2)}) async-start(bf16[4,1225,192]{1,2,0:T(8,128)(2,1)} %copy.244), calls=%async_computation.4 | async-start | bytes 3932160 | tf_op jit(solution)/shard_map/all_to_all | solution.py:95
  1022.2 29.3 %copy-start.68 = (bf16[1,16,768]{2,0,1:T(2,128)(2,1)S(1)}, bf16[1,16,768]{2,0,1:T(2,128)(2,1)}, u32[]{:S(2)}) copy-start(bf16[1,16,768]{2,0,1:T(2,128)(2,1)} %fusion.125) | copy-start | bytes 73732
  1023.7 27.9 %all-to-all-start.8 = ((bf16[4,1225,192]{1,2,0:T(8,128)(2,1)}), bf16[4,1225,192]{1,2,0:T(8,128)(2,1)S(1)}, u32[]{:S(2)}, u32[]{:S(2)}) async-start(bf16[4,1225,192]{1,2,0:T(8,128)(2,1)} %copy.253), calls=%async_computation.8 | async-start | bytes 3932160 | tf_op jit(solution)/shard_map/all_to_all | solution.py:107
  1062.4 14.9 slice-start
  1062.4 29.3 %all-to-all-start.9 = ((bf16[1225,4,192]{0,2,1:T(8,128)(2,1)}), bf16[1225,4,192]{0,2,1:T(8,128)(2,1)}, u32[]{:S(2)}, u32[]{:S(2)}) async-start(bf16[1225,4,192]{0,2,1:T(8,128)(2,1)} %bitcast.305), calls=%async_computation.9 | async-start | bytes 3932160 | tf_op jit(solution)/shard_map/all_to_all | solution.py:111
  1091.6 358.2 %all-to-all-start.5 = ((bf16[1225,4,192]{0,2,1:T(8,128)(2,1)}), bf16[1225,4,192]{0,2,1:T(8,128)(2,1)}, u32[]{:S(2)}, u32[]{:S(2)}) async-start(bf16[1225,4,192]{0,2,1:T(8,128)(2,1)} %bitcast.38), calls=%async_computation.5 | async-start | bytes 3932160 | tf_op jit(solution)/shard_map/all_to_all | solution.py:101
  1143.1 14.2 copy-start.10
  1257.1 94.8 %copy-start.66 = (bf16[14,14,64]{2,1,0:T(8,128)(2,1)S(1)}, bf16[14,14,64]{2,1,0:T(8,128)(2,1)}, u32[]{:S(2)}) copy-start(bf16[14,14,64]{2,1,0:T(8,128)(2,1)} %copy-done.65) | copy-start | bytes 75268
  1351.8 10.3 copy-start.14
  1351.8 10.3 copy-start.64
  1449.8 17.4 slice-start.2
  1449.8 72.1 %all-to-all-start.10 = ((bf16[4,1225,576]{1,2,0:T(8,128)(2,1)}), bf16[4,1225,576]{1,2,0:T(8,128)(2,1)}, u32[]{:S(2)}, u32[]{:S(2)}) async-start(bf16[4,1225,576]{1,2,0:T(8,128)(2,1)} %copy.267), calls=%async_computation.10 | async-start | bytes 11796480 | tf_op jit(solution)/shard_map/all_to_all | solution.py:107
  1485.0 37.0 %copy-start.52 = (bf16[1,16,2304]{2,0,1:T(2,128)(2,1)S(1)}, bf16[1,16,2304]{2,0,1:T(2,128)(2,1)}, u32[]{:S(2)}) copy-start(bf16[1,16,2304]{2,0,1:T(2,128)(2,1)} %copy-done.51) | copy-start | bytes 221188
  1540.4 33.6 %all-to-all-start.11 = ((bf16[1225,4,192]{0,2,1:T(8,128)(2,1)}), bf16[1225,4,192]{0,2,1:T(8,128)(2,1)}, u32[]{:S(2)}, u32[]{:S(2)}) async-start(bf16[1225,4,192]{0,2,1:T(8,128)(2,1)} %bitcast.303), calls=%async_computation.11 | async-start | bytes 3932160 | tf_op jit(solution)/shard_map/all_to_all | solution.py:115
  1544.9 174.2 %all-reduce.6.cloned.1.call-start = ((), (), s32[]{:S(2)}) async-start(), calls=%async_computation.18 | async-start | bytes 12582912 | tf_op jit(solution)/shard_map/psum | solution.py:339
  1602.8 130.2 %copy-start.1 = (bf16[27,64]{1,0:T(8,128)(2,1)S(1)}, bf16[27,64]{1,0:T(8,128)(2,1)}, u32[]{:S(2)}) copy-start(bf16[27,64]{1,0:T(8,128)(2,1)} %param.28) | copy-start | bytes 10372
  (68 other events, 435.6 us)
Sparse Core Ops, SparseCore 0:
  20.2 70.9 all-gather.6
  92.7 15.9 all-gather.14
  178.6 23.1 all-gather.10
  252.8 28.3 all-gather.8
  282.7 88.5 all-gather.16
  747.1 100.4 all-gather.12
  1556.5 162.6 all-reduce.5
